TPU v7x, 128 devices: a whole 4x4x4 slice. The times are simulated.
128 devices in a mesh: grid: 8 (over x, core), proc: 16 (over z, y).
Axes of the slice: x: 4, y: 4, z: 4, core: 2. Of those that a mesh axis runs over, the one named last changes fastest.
Arguments:
- rhs: float32 [3, 8, 16, 256, 1024], P(None, 'grid', 'proc'), may hold values from -6 to 6
- tile_pairs: int32 [2, 8, 16, 32], P(None, 'grid', 'proc'), may hold values from -1 to 31, as said below
- tiles: bfloat16 [2, 8, 16, 32, 256, 256], P(None, 'grid', 'proc'), may hold values from -0.09375 to 0.09375
- dinv: float32 [3, 8, 16, 256, 256], P(None, 'grid', 'proc'), as said below
Outputs:
- solution: float32 [3, 8, 16, 256, 1024], P(None, 'grid', 'proc')
Inputs may be any that keep to these rules, and one draw needn't show every extreme that they name: tile_pairs[t, g, p] holds distinct pair numbers in its first slots and -1 in the others; pair number q names block column q mod 16 and destination q // 16 (0: the same grid, 1: the partner grid). In every transition and grid one device uses all 32 slots and the others use 2 to 16 of them. Each dinv tile is lower triangular with diagonal entries between 0.5 and 1.4.
All inputs are finite; a program needn't handle non-finite values.
Results may differ from a plain program's by a relative error of at most 0.0021.
Values may be sent and summed in bfloat16 or wider, within the bound.
No kernel may reach another device: no remote copies, remote signals or barrier semaphores. Data moves between devices by JAX's collectives and lax.ppermute only.
A program may use at most 128 MiB of HBM per device.

v0:
```python
import jax
import jax.numpy as jnp
from jax import lax
from jax.sharding import PartitionSpec as P


def from_partner(block, axis, apart):
    count = lax.axis_size(axis)
    route = []
    for low in range(count):
        high = low | 1 << apart
        if high != low and high < count:
            route += [(low, high), (high, low)]
    return lax.ppermute(block, axis, route)


def build_table(pairs, tile_set):
    slot_count = tile_set.shape[0]
    labels = lax.broadcasted_iota(jnp.int32, (slot_count, slot_count), 1)
    onehot = (pairs[:, None] == labels).astype(jnp.bfloat16)
    dense = jnp.einsum("sq,sij->qij", onehot, tile_set, preferred_element_type=jnp.float32)
    return dense.astype(jnp.bfloat16).reshape(
        2, slot_count // 2, tile_set.shape[1], tile_set.shape[2]
    )


def diagonal_solve(factor, values):
    return jnp.dot(
        factor, values, precision=lax.Precision.HIGHEST, preferred_element_type=jnp.float32
    )


def solve_levels(rhs_block, dinv_block, tables):
    levels = rhs_block.shape[0]
    current = diagonal_solve(dinv_block[0], rhs_block[0])
    solved = [current]
    for height in range(1, levels):
        dense_table = tables[height - 1]
        outgoing = current.astype(jnp.bfloat16)[None]
        partial_value = jnp.einsum(
            "dkij,kjr->dir",
            dense_table,
            lax.all_gather(outgoing, "proc", axis=0, tiled=True),
            preferred_element_type=jnp.float32,
        )
        partner = from_partner(partial_value[1], "grid", height - 1)
        update = partial_value[0] + partner
        current = diagonal_solve(dinv_block[height], rhs_block[height] - update)
        solved.append(current)
    return jnp.stack(solved)


def body(rhs, tile_pairs, tiles, dinv):
    rhs_block = rhs[:, 0, 0]
    dinv_block = dinv[:, 0, 0]
    tables = [
        build_table(tile_pairs[number, 0, 0], tiles[number, 0, 0])
        for number in range(tile_pairs.shape[0])
    ]
    solved = solve_levels(rhs_block, dinv_block, tables)
    return solved[:, None, None]


def solution(mesh):
    return jax.shard_map(
        body,
        mesh=mesh,
        in_specs=(
            P(None, "grid", "proc", None, None),
            P(None, "grid", "proc", None),
            P(None, "grid", "proc", None, None, None),
            P(None, "grid", "proc", None, None),
        ),
        out_specs=P(None, "grid", "proc", None, None),
        check_vma=False,
    )
```

profile of v0, /device:TPU:0, one launch (start us, length us, event | category | flops | bytes accessed | tf_op | source)
XLA Modules:
  0.0 222.2 jit_solution(5536468738525607536)
XLA Ops:
  6.5 0.0 all-gather.5.cloned.1.call-start
  6.5 3.1 %fusion.41 = (bf16[256,1024]{1,0:T(8,128)(2,1)}, f32[256,1024]{1,0:T(8,128)S(1)}) fusion(f32[3,1,1,256,1024]{4,3,2,1,0:T(8,128)} %param.4, f32[3,1,1,256,256]{4,3,2,1,0:T(8,128)} %param.7), kind=kOutput, calls=%fused_computation.46 | convolution fusion | flops 805568512 | bytes 2883584 | tf_op jit(solution)/shard_map/dot_general | solution.py:28
  9.7 0.0 all-gather.5.cloned.1.call-update
  9.7 0.0 all-gather.7.cloned.1.call-start
  9.7 0.7 slice_bitcast_fusion.4
  10.4 5.2 %fusion.40 = (bf16[1,1,1,32,256,256]{5,4,3,2,1,0:T(8,128)(2,1)}, bf16[1,1,1,32,256,256]{5,4,3,2,1,0:T(8,128)(2,1)S(1)}) fusion(bf16[2,1,1,32,256,256]{5,4,3,2,1,0:T(8,128)(2,1)} %param.6), kind=kLoop, calls=%fused_computation.45 | loop fusion | bytes 16777216 | tf_op jit(solution)/shard_map/slice | solution.py:57
  15.6 4.6 %fusion.6 = bf16[32,256,256]{2,0,1:T(8,128)(2,1)} fusion(bf16[1,1,1,32,256,256]{5,4,3,2,1,0:T(8,128)(2,1)S(1)} %get-tuple-element.6, s32[32]{0:T(128)S(1)} %get-tuple-element.8), kind=kOutput, calls=%fused_computation.9 | convolution fusion | flops 136315904 | bytes 8388736 | tf_op jit(solution)/shard_map/sq,sij->qij/dot_general | solution.py:21
  20.2 63.1 %all-gather.5.cloned.1.call-done = bf16[4096,1024]{1,0:T(8,128)(2,1)} async-done(((bf16[256,1024]{1,0:T(8,128)(2,1)}), bf16[4096,1024]{1,0:T(8,128)(2,1)}) %all-gather.5.cloned.1.call-update) | async-done | bytes 8388624 | tf_op jit(solution)/shard_map/all_gather | solution.py:43
  83.3 0.0 copy-start
  83.3 13.0 %fusion.8 = f32[2,256,1024]{2,1,0:T(8,128)S(1)} fusion(bf16[16,256,1024,1]{2,1,0,3:T(8,128)(2,1)} %bitcast.103, bf16[2,16,256,256]{3,1,0,2:T(8,128)(2,1)} %bitcast.99), kind=kOutput, calls=%fused_computation.11 | convolution fusion | flops 4294967296 | bytes 14680064 | tf_op jit(solution)/shard_map/dkij,kjr->dir/dot_general | solution.py:40
  96.3 0.1 slice_bitcast_fusion.2
  96.4 0.3 collective-permute-start
  96.6 2.6 %collective-permute-done = f32[256,1024]{1,0:T(8,128)S(1)} collective-permute-done((f32[256,1024]{1,0:T(8,128)S(1)}, f32[256,1024]{1,0:T(8,128)S(1)}, u32[]{:S(2)}, u32[]{:S(2)}) %collective-permute-start) | collective-permute-done | bytes 1048608 | tf_op jit(solution)/shard_map/ppermute | solution.py:14
  99.3 0.0 copy-done
  99.3 3.2 %bitcast_convert_fusion = (bf16[256,1024]{1,0:T(8,128)(2,1)}, f32[1024,256]{0,1:T(8,128)S(1)}) fusion(f32[3,1,1,256,256]{4,3,2,1,0:T(8,128)S(1)} %copy-done, f32[256,1024]{1,0:T(8,128)S(1)} %collective-permute-done, f32[2,256,1024]{2,1,0:T(8,128)S(1)} %fusion.8, f32[3,1,1,256,1024]{4,3,2,1,0:T(8,128)} %param.4), kind=kOutput, calls=%fused_computation.24 | convolution fusion | flops 806092800 | bytes 4980736 | tf_op jit(solution)/shard_map/dot_general | solution.py:28
  102.5 0.0 all-gather.7.cloned.1.call-update
  102.5 6.8 %fusion.7 = bf16[32,256,256]{2,0,1:T(8,128)(2,1)} fusion(bf16[1,1,1,32,256,256]{5,4,3,2,1,0:T(8,128)(2,1)} %get-tuple-element.5, s32[32]{0:T(128)S(1)} %get-tuple-element.7), kind=kOutput, calls=%fused_computation.10 | convolution fusion | flops 136315904 | bytes 8388736 | tf_op jit(solution)/shard_map/sq,sij->qij/dot_general | solution.py:21
  109.3 63.9 %all-gather.7.cloned.1.call-done = bf16[4096,1024]{1,0:T(8,128)(2,1)} async-done(((bf16[256,1024]{1,0:T(8,128)(2,1)}), bf16[4096,1024]{1,0:T(8,128)(2,1)}) %all-gather.7.cloned.1.call-update) | async-done | bytes 8388624 | tf_op jit(solution)/shard_map/all_gather | solution.py:43
  173.2 12.9 %fusion.11 = f32[2,256,1024]{2,1,0:T(8,128)S(1)} fusion(bf16[16,256,1024,1]{2,1,0,3:T(8,128)(2,1)} %bitcast.104, bf16[2,16,256,256]{3,1,0,2:T(8,128)(2,1)} %bitcast.100), kind=kOutput, calls=%fused_computation.12 | convolution fusion | flops 4294967296 | bytes 14680064 | tf_op jit(solution)/shard_map/dkij,kjr->dir/dot_general | solution.py:40
  186.1 0.1 slice_bitcast_fusion
  186.2 1.5 collective-permute-start.1
  187.8 23.3 %collective-permute-done.1 = f32[256,1024]{1,0:T(8,128)S(1)} collective-permute-done((f32[256,1024]{1,0:T(8,128)S(1)}, f32[256,1024]{1,0:T(8,128)S(1)}, u32[]{:S(2)}, u32[]{:S(2)}) %collective-permute-start.1) | collective-permute-done | bytes 1048608 | tf_op jit(solution)/shard_map/ppermute | solution.py:14
  211.0 2.4 %convolution_bitcast_fusion = f32[1,256,1024]{2,1,0:T(8,128)S(1)} fusion(f32[256,1024]{1,0:T(8,128)S(1)} %collective-permute-done.1, f32[2,256,1024]{2,1,0:T(8,128)S(1)} %fusion.11, f32[3,1,1,256,1024]{4,3,2,1,0:T(8,128)} %param.4, f32[3,1,1,256,256]{4,3,2,1,0:T(8,128)S(1)} %copy-done), kind=kOutput, calls=%fused_computation.13 | convolution fusion | flops 805830656 | bytes 4456448 | tf_op jit(solution)/shard_map/dot_general | solution.py:28
  213.5 1.9 maximum_bitcast_fusion
Async XLA Ops:
  6.5 76.7 %all-gather.5.cloned.1.call-start = ((), (), s32[]{:S(2)}) async-start(), calls=%async_computation | async-start | bytes 8912896 | tf_op jit(solution)/shard_map/all_gather | solution.py:43
  9.7 163.5 %all-gather.7.cloned.1.call-start = ((), (), s32[]{:S(2)}) async-start(), calls=%async_computation.1 | async-start | bytes 8912896 | tf_op jit(solution)/shard_map/all_gather | solution.py:43
  83.3 16.0 %copy-start = (f32[3,1,1,256,256]{4,3,2,1,0:T(8,128)S(1)}, f32[3,1,1,256,256]{4,3,2,1,0:T(8,128)}, u32[]{:S(2)}) copy-start(f32[3,1,1,256,256]{4,3,2,1,0:T(8,128)} %param.7) | copy-start | bytes 2359300
  96.4 2.9 %collective-permute-start = (f32[256,1024]{1,0:T(8,128)S(1)}, f32[256,1024]{1,0:T(8,128)S(1)}, u32[]{:S(2)}, u32[]{:S(2)}) collective-permute-start(f32[256,1024]{1,0:T(8,128)S(1)} %slice_bitcast_fusion.2), channel_id=1, source_target_pairs={{0,16},{16,0},{32,48},{48,32},{64,80},{80,64},{96,112},{112,96},{1... | collective-permute-start | bytes 3145736 | tf_op jit(solution)/shard_map/ppermute | solution.py:14
  186.2 24.8 %collective-permute-start.1 = (f32[256,1024]{1,0:T(8,128)S(1)}, f32[256,1024]{1,0:T(8,128)S(1)}, u32[]{:S(2)}, u32[]{:S(2)}) collective-permute-start(f32[256,1024]{1,0:T(8,128)S(1)} %slice_bitcast_fusion), channel_id=1, source_target_pairs={{0,32},{32,0},{16,48},{48,16},{64,96},{96,64},{80,112},{112,80},{1... | collective-permute-start | bytes 3145736 | tf_op jit(solution)/shard_map/ppermute | solution.py:14
Sparse Core Ops, SparseCore 0:
  9.8 73.4 all-gather.4
  102.6 70.5 all-gather.6
where the time goes:
time: 222 us
  waiting for transfers between devices  153 us (69%)
  matrix products  45.9 us (21%)
  between operations  13.5 us (6%)
  local copies, waits for them, and re-layouts  6.09 us (3%)
    all_gather x2, waiting for transfers between devices, solve_levels(): lax.all_gather(outgoing, 'proc', axis=0, tiled=True)  127 us
    ppermute x2, waiting for transfers between devices, from_partner(): return lax.ppermute(block, axis, route)  25.9 us
    dot_general x2, matrix products, solve_levels(): jnp.einsum('dkij,kjr->dir', dense_table, lax.all_gather(outgoing, 'proc',...  25.9 us
    dot_general x2, matrix products, build_table(): jnp.einsum('sq,sij->qij', onehot, tile_set, preferred_element_type=jnp.fl...  11.3 us
    dot_general x3, matrix products, diagonal_solve(): jnp.dot(factor, values, precision=lax.Precision.HIGHEST, preferred_elemen...  8.76 us
    slice x1, local copies, waits for them, and re-layouts, body(): tiles[number, 0, 0]  5.2 us
  transfers between devices with their start and end apart: 4, of which 4 were waited for; matrix products, arithmetic and copies ran while one was open for 8% of the time, Pallas kernels for 0%

commit v1 on v0

--- a/solution.py
+++ b/solution.py
@@ -40,7 +40,9 @@
         partial_value = jnp.einsum(
             "dkij,kjr->dir",
             dense_table,
-            lax.all_gather(outgoing, "proc", axis=0, tiled=True),
+            jnp.concatenate(
+                lax.all_to_all(jnp.stack([outgoing] * lax.axis_size("proc")), "proc", 0, 0), axis=0
+            ),
             preferred_element_type=jnp.float32,
         )
         partner = from_partner(partial_value[1], "grid", height - 1)

time: 222 us -> 335 us (1.51)
  waiting for transfers between devices: 153 us -> 258 us
  starting transfers between devices: 1.86 us -> 15.8 us
  between operations: 13.5 us -> 0.1 us
  local copies, waits for them, and re-layouts: 6.09 us -> 14.1 us
    all_to_all x0 -> x2, waiting for transfers between devices: none -> 233 us  [solve_levels(): lax.all_to_all(jnp.stack([outgoing] * lax.axis_size('proc')), 'proc', 0, 0)]
    all_gather x2 -> x0, waiting for transfers between devices: 127 us -> none  [solve_levels(): lax.all_gather(outgoing, 'proc', axis=0, tiled=True)]
    all_to_all x0 -> x2, starting transfers between devices: none -> 14 us  [solve_levels(): lax.all_to_all(jnp.stack([outgoing] * lax.axis_size('proc')), 'proc', 0, 0)]
    another operation x0 -> x2, local copies, waits for them, and re-layouts: none -> 8.68 us  [solve_levels(): jnp.stack([outgoing] * lax.axis_size('proc'))]
  transfers between devices with their start and end apart: 4 -> 4, of which waited for: 4 -> 4; matrix products, arithmetic and copies ran while one was open for 8% -> 5% of each run, Pallas kernels for 0% -> 0%
where the time goes in v1:
time: 335 us; the launch traced here: 334 us
  waiting for transfers between devices  258 us (77%)
  matrix products  44.5 us (13%)
  starting transfers between devices  15.8 us (5%)
  local copies, waits for them, and re-layouts  14.1 us (4%)
    all_to_all x2, waiting for transfers between devices, solve_levels(): lax.all_to_all(jnp.stack([outgoing] * lax.axis_size('proc')), 'proc', 0, 0)  233 us
    dot_general x2, matrix products, solve_levels(): jnp.einsum('dkij,kjr->dir', dense_table, jnp.concatenate(lax.all_to_all(j...  25.9 us
    ppermute x2, waiting for transfers between devices, from_partner(): return lax.ppermute(block, axis, route)  25.3 us
    all_to_all x2, starting transfers between devices, solve_levels(): lax.all_to_all(jnp.stack([outgoing] * lax.axis_size('proc')), 'proc', 0, 0)  14 us
    dot_general x2, matrix products, build_table(): jnp.einsum('sq,sij->qij', onehot, tile_set, preferred_element_type=jnp.fl...  11.4 us
    another operation x2, local copies, waits for them, and re-layouts, solve_levels(): jnp.stack([outgoing] * lax.axis_size('proc'))  8.68 us
    dot_general x3, matrix products, diagonal_solve(): jnp.dot(factor, values, precision=lax.Precision.HIGHEST, preferred_elemen...  7.18 us
  transfers between devices with their start and end apart: 4, of which 4 were waited for; matrix products, arithmetic and copies ran while one was open for 5% of the time, Pallas kernels for 0%

profile of v1, /device:TPU:0, one launch (start us, length us, event | category | flops | bytes accessed | tf_op | source)
XLA Modules:
  0.0 334.4 jit_solution(13057985138132216624)
XLA Ops:
  0.0 2.3 fusion.47
  2.3 4.3 %stack.19 = bf16[16,1,256,1024]{3,2,1,0:T(8,128)(2,1)} broadcast(bf16[256,1024]{1,0:T(8,128)(2,1)S(1)} %get-tuple-element.9), dimensions={2,3} | broadcast | bytes 8912896 | tf_op jit(solution)/shard_map/stack | solution.py:44
  6.7 0.0 copy-start.1
  6.7 8.3 %all-to-all-start = ((bf16[16,1,256,1024]{3,2,1,0:T(8,128)(2,1)}), bf16[16,1,256,1024]{3,2,1,0:T(8,128)(2,1)}, u32[]{:S(2)}, u32[]{:S(2)}) async-start(bf16[16,1,256,1024]{3,2,1,0:T(8,128)(2,1)} %stack.19), calls=%async_computation | async-start | bytes 16777216 | tf_op jit(solution)/shard_map/all_to_all | solution.py:44
  15.0 0.0 copy-done.1
  15.1 5.2 %fusion.46 = (bf16[1,1,1,32,256,256]{5,4,3,2,1,0:T(8,128)(2,1)}, bf16[1,1,1,32,256,256]{5,4,3,2,1,0:T(8,128)(2,1)S(1)}) fusion(bf16[2,1,1,32,256,256]{5,4,3,2,1,0:T(8,128)(2,1)} %param.6), kind=kLoop, calls=%fused_computation.47 | loop fusion | bytes 16777216 | tf_op jit(solution)/shard_map/slice | solution.py:59
  20.3 4.6 %fusion.8 = bf16[32,256,256]{2,0,1:T(8,128)(2,1)} fusion(bf16[1,1,1,32,256,256]{5,4,3,2,1,0:T(8,128)(2,1)S(1)} %get-tuple-element.6, s32[32]{0:T(128)S(1)} %get-tuple-element.8), kind=kOutput, calls=%fused_computation.11 | convolution fusion | flops 136315904 | bytes 8388736 | tf_op jit(solution)/shard_map/sq,sij->qij/dot_general | solution.py:21
  24.9 114.3 %all-to-all-done = bf16[16,1,256,1024]{3,2,1,0:T(8,128)(2,1)} async-done(((bf16[16,1,256,1024]{3,2,1,0:T(8,128)(2,1)}), bf16[16,1,256,1024]{3,2,1,0:T(8,128)(2,1)}, u32[]{:S(2)}, u32[]{:S(2)}) %all-to-all-start) | async-done | bytes 8388640 | tf_op jit(solution)/shard_map/all_to_all | solution.py:44
  139.2 0.0 copy-start
  139.2 13.0 %fusion.10 = f32[2,256,1024]{2,1,0:T(8,128)S(1)} fusion(bf16[16,1,256,1024]{3,2,1,0:T(8,128)(2,1)} %all-to-all-done, bf16[2,16,256,256]{3,1,0,2:T(8,128)(2,1)} %bitcast.103), kind=kOutput, calls=%fused_computation.13 | convolution fusion | flops 4294967296 | bytes 14680064 | tf_op jit(solution)/shard_map/dkij,kjr->dir/dot_general | solution.py:40
  152.2 0.1 slice_bitcast_fusion.2
  152.3 0.3 collective-permute-start
  152.5 2.6 collective-permute-done
  155.2 0.0 copy-done
  155.2 2.4 bitcast_convert_fusion
  157.6 4.3 %stack.21 = bf16[16,1,256,1024]{3,2,1,0:T(8,128)(2,1)} broadcast(bf16[256,1024]{1,0:T(8,128)(2,1)S(1)} %get-tuple-element.11), dimensions={2,3} | broadcast | bytes 8912896 | tf_op jit(solution)/shard_map/stack | solution.py:44
  162.0 5.7 %all-to-all-start.1 = ((bf16[16,1,256,1024]{3,2,1,0:T(8,128)(2,1)}), bf16[16,1,256,1024]{3,2,1,0:T(8,128)(2,1)}, u32[]{:S(2)}, u32[]{:S(2)}) async-start(bf16[16,1,256,1024]{3,2,1,0:T(8,128)(2,1)} %stack.21), calls=%async_computation.1 | async-start | bytes 16777216 | tf_op jit(solution)/shard_map/all_to_all | solution.py:44
  167.6 6.8 %fusion.9 = bf16[32,256,256]{2,0,1:T(8,128)(2,1)} fusion(bf16[1,1,1,32,256,256]{5,4,3,2,1,0:T(8,128)(2,1)} %get-tuple-element.5, s32[32]{0:T(128)S(1)} %get-tuple-element.7), kind=kOutput, calls=%fused_computation.12 | convolution fusion | flops 136315904 | bytes 8388736 | tf_op jit(solution)/shard_map/sq,sij->qij/dot_general | solution.py:21
  174.4 118.5 %all-to-all-done.1 = bf16[16,1,256,1024]{3,2,1,0:T(8,128)(2,1)} async-done(((bf16[16,1,256,1024]{3,2,1,0:T(8,128)(2,1)}), bf16[16,1,256,1024]{3,2,1,0:T(8,128)(2,1)}, u32[]{:S(2)}, u32[]{:S(2)}) %all-to-all-start.1) | async-done | bytes 8388640 | tf_op jit(solution)/shard_map/all_to_all | solution.py:44
  292.9 12.9 %fusion.15 = f32[2,256,1024]{2,1,0:T(8,128)S(1)} fusion(bf16[16,1,256,1024]{3,2,1,0:T(8,128)(2,1)} %all-to-all-done.1, bf16[2,16,256,256]{3,1,0,2:T(8,128)(2,1)} %bitcast.104), kind=kOutput, calls=%fused_computation.14 | convolution fusion | flops 4294967296 | bytes 14680064 | tf_op jit(solution)/shard_map/dkij,kjr->dir/dot_general | solution.py:40
  305.8 0.1 slice_bitcast_fusion
  305.9 1.6 collective-permute-start.1
  307.5 22.6 %collective-permute-done.1 = f32[256,1024]{1,0:T(8,128)S(1)} collective-permute-done((f32[256,1024]{1,0:T(8,128)S(1)}, f32[256,1024]{1,0:T(8,128)S(1)}, u32[]{:S(2)}, u32[]{:S(2)}) %collective-permute-start.1) | collective-permute-done | bytes 1048608 | tf_op jit(solution)/shard_map/ppermute | solution.py:14
  330.1 2.4 convolution_bitcast_fusion
  332.6 1.9 maximum_bitcast_fusion
  (1 shorter events, 0.0 us)
Async XLA Ops:
  6.7 8.4 %copy-start.1 = (s32[2,1,1,32]{3,2,1,0:T(1,128)S(1)}, s32[2,1,1,32]{3,2,1,0:T(1,128)}, u32[]{:S(2)}) copy-start(s32[2,1,1,32]{3,2,1,0:T(1,128)} %param.5) | copy-start | bytes 772
  6.7 132.5 %all-to-all-start = ((bf16[16,1,256,1024]{3,2,1,0:T(8,128)(2,1)}), bf16[16,1,256,1024]{3,2,1,0:T(8,128)(2,1)}, u32[]{:S(2)}, u32[]{:S(2)}) async-start(bf16[16,1,256,1024]{3,2,1,0:T(8,128)(2,1)} %stack.19), calls=%async_computation | async-start | bytes 16777216 | tf_op jit(solution)/shard_map/all_to_all | solution.py:44
  139.2 16.0 %copy-start = (f32[3,1,1,256,256]{4,3,2,1,0:T(8,128)S(1)}, f32[3,1,1,256,256]{4,3,2,1,0:T(8,128)}, u32[]{:S(2)}) copy-start(f32[3,1,1,256,256]{4,3,2,1,0:T(8,128)} %param.7) | copy-start | bytes 2359300
  152.3 2.9 collective-permute-start
  162.0 131.0 %all-to-all-start.1 = ((bf16[16,1,256,1024]{3,2,1,0:T(8,128)(2,1)}), bf16[16,1,256,1024]{3,2,1,0:T(8,128)(2,1)}, u32[]{:S(2)}, u32[]{:S(2)}) async-start(bf16[16,1,256,1024]{3,2,1,0:T(8,128)(2,1)} %stack.21), calls=%async_computation.1 | async-start | bytes 16777216 | tf_op jit(solution)/shard_map/all_to_all | solution.py:44
  305.9 24.2 %collective-permute-start.1 = (f32[256,1024]{1,0:T(8,128)S(1)}, f32[256,1024]{1,0:T(8,128)S(1)}, u32[]{:S(2)}, u32[]{:S(2)}) collective-permute-start(f32[256,1024]{1,0:T(8,128)S(1)} %slice_bitcast_fusion), channel_id=1, source_target_pairs={{0,32},{32,0},{16,48},{48,16},{64,96},{96,64},{80,112},{112,80},{1... | collective-permute-start | bytes 3145736 | tf_op jit(solution)/shard_map/ppermute | solution.py:14
